TPU v7x, 32 devices: a whole 2x2x4 slice. The times are simulated.
32 devices in a mesh: dp: 16 (over z, x, core), rep: 2 (over y).
Axes of the slice: x: 2, y: 2, z: 4, core: 2. Of those that a mesh axis runs over, the one named last changes fastest.
Arguments:
- learn_residual: bfloat16 [20480, 1024], P(('dp', 'rep')), may hold values from -6 to 6
- learn_hidden: bfloat16 [20480, 4096], P(('dp', 'rep')), may hold values from -6 to 6
- fresh_residual: bfloat16 [20480, 1024], P(('dp', 'rep')), may hold values from -6 to 6
- fresh_hidden: bfloat16 [20480, 4096], P(('dp', 'rep')), may hold values from -6 to 6
- down_weight: bfloat16 [4096, 1024], P('dp'), may hold values from -0.09375 to 0.09375
- head_weight: bfloat16 [1024, 19], replicated, may hold values from -0.1875 to 0.1875
- norm_gain: bfloat16 [1024], replicated, may hold values from 0.099609375 to 1.8984375
- actions: int32 [256, 80], P(('dp', 'rep')), may hold values from 0 to 17
- behaviour_logits: float32 [20480, 18], P(('dp', 'rep')), may hold values from -6 to 6
- rewards: float32 [256, 80], P(('dp', 'rep')), may hold values from -6 to 6
- episode_done: int32 [256, 80], P(('dp', 'rep')), may hold values 0 or 1
- lengths: int32 [256], P(('dp', 'rep')), may hold values from 40 to 80, as said below
- bootstrap: float32 [256], P(('dp', 'rep')), may hold values from -6 to 6
Outputs:
- fresh_policy: float32 [20480, 19], P(('dp', 'rep'))
- learn_targets: float32 [256, 80], P(('dp', 'rep'))
- hidden_grad: bfloat16 [20480, 4096], P(('dp', 'rep'))
- down_grad: float32 [4096, 1024], P('dp')
- head_grad: float32 [1024, 19], replicated
- gain_grad: float32 [1024], replicated
Inputs may be any that keep to these rules, and one draw needn't show every extreme that they name: `lengths`: on at least one device all 8 trajectories of that device have the full 80 steps.
All inputs are finite; a program needn't handle non-finite values. No bound on the sum of `episode_done` on one device may be relied on, other than what follows from the above.
Results may differ from a plain program's by a relative error of at most 0.0049.
Values may be sent and summed in bfloat16 or wider, within the bound.
A program may use at most 128 MiB of HBM per device.

v0:
```python
import jax
import jax.numpy as jnp
from jax import lax
from jax.sharding import PartitionSpec as P

ACTIONS = 18
STEPS = 80
TRAJ_DEV = 8
DISCOUNT = 0.99
BASELINE_COST = 0.5
ENTROPY_COST = 0.05
EPSILON = 1e-05


def normalize(features, gain_vector):
    inverse_rms = lax.rsqrt(jnp.mean(features * features, axis=1, keepdims=True) + EPSILON)
    return features * inverse_rms * gain_vector[None, :]


def head_outputs(features, head_matrix, gain_vector):
    return jnp.dot(normalize(features, gain_vector), head_matrix, precision=lax.Precision.HIGHEST)


def log_policy(logits):
    return logits - jnp.log(jnp.sum(jnp.exp(logits), axis=-1, keepdims=True))


def compose_steps(earlier, later):
    return (earlier[0] * later[0], later[1] + later[0] * earlier[1])


def trace_returns(errors, traces):
    _, corrections = lax.associative_scan(compose_steps, (traces, errors), reverse=True, axis=1)
    return corrections


def learner_loss(
    features,
    head_matrix,
    gain_vector,
    actions,
    behaviour_logits,
    rewards,
    episode_done,
    lengths,
    bootstrap,
):
    trajectories = actions.shape[0]
    outputs = head_outputs(features, head_matrix, gain_vector)
    logprob = log_policy(outputs[:, :ACTIONS])
    values = outputs[:, ACTIONS].reshape(trajectories, STEPS)
    one_hot = (
        actions.reshape(-1)[:, None] == jnp.arange(ACTIONS, dtype=jnp.int32)[None, :]
    ).astype(jnp.float32)
    taken = jnp.sum(logprob * one_hot, axis=1).reshape(trajectories, STEPS)
    behaved = jnp.sum(log_policy(behaviour_logits) * one_hot, axis=1).reshape(trajectories, STEPS)
    entropy = -jnp.sum(jnp.exp(logprob) * logprob, axis=1).reshape(trajectories, STEPS)
    clipped_ratio = jnp.minimum(1.0, jnp.exp(lax.stop_gradient(taken) - behaved))
    positions = jnp.arange(STEPS, dtype=jnp.int32)[None, :]
    inside = positions < lengths[:, None]
    final_step = positions == lengths[:, None] - 1
    discounts = DISCOUNT * (1.0 - episode_done.astype(jnp.float32))
    baseline = lax.stop_gradient(values)
    empty_column = jnp.zeros((trajectories, 1), jnp.float32)
    next_value = jnp.concatenate([baseline[:, 1:], empty_column], axis=1)
    next_value = jnp.where(final_step, bootstrap[:, None], next_value)
    errors = jnp.where(inside, clipped_ratio * (rewards + discounts * next_value - baseline), 0.0)
    traces = jnp.where(inside, discounts * clipped_ratio, 0.0)
    targets = baseline + trace_returns(errors, traces)
    next_target = jnp.concatenate([targets[:, 1:], empty_column], axis=1)
    next_target = jnp.where(final_step, bootstrap[:, None], next_target)
    advantage = clipped_ratio * (rewards + discounts * next_target - baseline)
    per_step = (
        -advantage * taken + 0.5 * BASELINE_COST * (targets - values) ** 2 - ENTROPY_COST * entropy
    )
    total_loss = jnp.sum(jnp.where(inside, per_step, 0.0)) / (TRAJ_DEV * STEPS)
    return (total_loss, targets)


def local(
    learn_residual,
    learn_hidden,
    fresh_residual,
    fresh_hidden,
    down_weight,
    head_weight,
    norm_gain,
    actions,
    behaviour_logits,
    rewards,
    episode_done,
    lengths,
    bootstrap,
):
    head_matrix = head_weight.astype(jnp.float32)
    gain_vector = norm_gain.astype(jnp.float32)
    full_down = lax.all_gather(down_weight, "dp", axis=0, tiled=True)
    learn_stream = learn_residual.astype(jnp.float32) + jnp.dot(
        learn_hidden, full_down, preferred_element_type=jnp.float32
    )
    fresh_stream = fresh_residual.astype(jnp.float32) + jnp.dot(
        fresh_hidden, full_down, preferred_element_type=jnp.float32
    )
    fresh_policy = head_outputs(fresh_stream, head_matrix, gain_vector)

    def loss_of(features, head_values, gain_values):
        return learner_loss(
            features,
            head_values,
            gain_values,
            actions,
            behaviour_logits,
            rewards,
            episode_done,
            lengths,
            bootstrap,
        )

    total_loss, pullback, targets = jax.vjp(
        loss_of, learn_stream, head_matrix, gain_vector, has_aux=True
    )
    stream_grad, head_local, gain_local = pullback(jnp.ones_like(total_loss))
    rounded = stream_grad.astype(jnp.bfloat16)
    head_grad, gain_grad = lax.psum((head_local, gain_local), ("dp", "rep"))
    grad_shard = lax.psum_scatter(
        lax.dot_general(
            learn_hidden, rounded, (((0,), (0,)), ((), ())), preferred_element_type=jnp.float32
        ),
        "dp",
        scatter_dimension=0,
        tiled=True,
    )
    down_grad = lax.psum(grad_shard, "rep")
    hidden_sum = lax.dot_general(
        rounded, full_down, (((1,), (1,)), ((), ())), preferred_element_type=jnp.float32
    )
    hidden_grad = hidden_sum.astype(jnp.bfloat16)
    return (fresh_policy, targets, hidden_grad, down_grad, head_grad, gain_grad)


def solution(mesh):
    placed = (
        P(("dp", "rep"), None),
        P(("dp", "rep"), None),
        P(("dp", "rep"), None),
        P(("dp", "rep"), None),
        P("dp", None),
        P(),
        P(),
        P(("dp", "rep"), None),
        P(("dp", "rep"), None),
        P(("dp", "rep"), None),
        P(("dp", "rep"), None),
        P(("dp", "rep")),
        P(("dp", "rep")),
    )
    return jax.shard_map(
        local,
        mesh=mesh,
        in_specs=placed,
        out_specs=(
            P(("dp", "rep"), None),
            P(("dp", "rep"), None),
            P(("dp", "rep"), None),
            P("dp", None),
            P(),
            P(),
        ),
        check_vma=False,
    )
```

profile of v0, /device:TPU:8, one launch (start us, length us, event | category | flops | bytes accessed | tf_op | source)
XLA Modules:
  0.0 475.9 jit_solution(9676328896604979801)
XLA Ops:
  7.2 0.7 all-gather.2.cloned.1.call-update
  8.0 0.7 convert_element_type.21
  8.6 0.8 eq.12
  9.4 0.9 exponential_reduce_fusion
  10.3 0.7 broadcast_add_fusion
  10.9 74.4 %all-gather.2.cloned.1.call-done = bf16[4096,1024]{1,0:T(8,128)(2,1)} async-done(((bf16[256,1024]{1,0:T(8,128)(2,1)}), bf16[4096,1024]{1,0:T(8,128)(2,1)}) %all-gather.2.cloned.1.call-update) | async-done | bytes 8388624 | tf_op jit(solution)/shard_map/all_gather | solution.py:97
  85.4 9.9 %multiply_reduce_fusion.2 = (f32[640]{0:T(1024)S(1)}, f32[640,1024]{1,0:T(8,128)S(1)}) fusion(bf16[640,4096]{1,0:T(8,128)(2,1)} %param.14, bf16[4096,1024]{1,0:T(8,128)(2,1)} %all-gather.2.cloned.1.call-done, bf16[640,1024]{1,0:T(8,128)(2,1)} %param.13), kind=kOutput, calls=%fused_computation.6 | convolution fusion | flops 5371330048 | bytes 17566208 | tf_op jit(solution)/shard_map/dot_general | solution.py:98
  95.4 1.5 fusion.6
  97.4 0.1 slice.177
  97.5 0.1 slice.171
  97.6 0.1 slice.167
  97.7 0.1 slice.173
  97.8 0.1 slice.169
  98.2 0.1 slice.185
  100.2 0.1 slice.176
  100.3 0.1 slice.165
  101.7 0.1 pad.56
  102.0 0.1 pad.55
  102.7 1.8 multiply_reduce_fusion
  104.6 0.5 fusion
  105.1 1.2 copy-done.1
  106.3 12.7 %convolution_bitcast_fusion = f32[4096,1024]{0,1:T(8,128)} fusion(bf16[640,1024]{1,0:T(8,128)(2,1)S(1)} %fusion, bf16[640,4096]{1,0:T(8,128)(2,1)} %param.14), kind=kOutput, calls=%fused_computation | convolution fusion | flops 5368709120 | bytes 23330816 | tf_op jit(solution)/shard_map/dot_general | solution.py:126
  119.0 175.0 %reduce-scatter.2.cloned.1.call-done = f32[256,1024]{0,1:T(8,128)} async-done(((f32[4096,1024]{0,1:T(8,128)}), f32[256,1024]{0,1:T(8,128)}) %reduce-scatter.2.cloned.1.call-update) | async-done | bytes 1048592 | tf_op jit(solution)/shard_map/reduce_scatter | solution.py:125
  294.1 0.2 all-reduce.21.cloned.1.call-start
  294.3 10.9 %multiply_reduce_fusion.3 = (f32[640]{0:T(1024)S(1)}, f32[640,1024]{1,0:T(8,128)}) fusion(bf16[640,1024]{1,0:T(8,128)(2,1)} %param.15, bf16[640,4096]{1,0:T(8,128)(2,1)} %param.16, bf16[4096,1024]{1,0:T(8,128)(2,1)} %all-gather.2.cloned.1.call-done), kind=kOutput, calls=%fused_computation.11 | convolution fusion | flops 5371330048 | bytes 17566208 | tf_op jit(solution)/shard_map/dot_general | solution.py:101
  305.2 2.4 fusion.4
  307.6 11.1 %convolution_convert_fusion = bf16[640,4096]{1,0:T(8,128)(2,1)} fusion(bf16[640,1024]{1,0:T(8,128)(2,1)} %copy-done.1, bf16[4096,1024]{1,0:T(8,128)(2,1)} %all-gather.2.cloned.1.call-done), kind=kOutput, calls=%fused_computation.1 | convolution fusion | flops 5371330560 | bytes 14942208 | tf_op jit(solution)/shard_map/dot_general | solution.py:134
  318.8 2.3 fusion.1
  321.1 40.5 %psum.23 = f32[1024]{0:T(1024)} all-reduce(f32[1024]{0:T(1024)S(1)} %get-tuple-element.12), channel_id=1, replica_groups=mesh['dp'=16,'rep'=2] {'dp','rep'}, use_global_device_ids=true, to_apply=%region_12.13 | all-reduce | flops 1024 | bytes 8192 | tf_op jit(solution)/shard_map/psum | solution.py:124
  361.5 2.5 copy.19
  364.1 103.8 %all-reduce.21.cloned.1.call-done = f32[1024,19]{0,1:T(8,128)} async-done(((f32[1024,19]{0,1:T(8,128)}), f32[1024,19]{0,1:T(8,128)}) %all-reduce.21.cloned.1.call-update) | async-done | bytes 77840 | tf_op jit(solution)/shard_map/psum | solution.py:124
  467.8 1.5 copy.22
  (107 shorter events, 4.8 us)
Async XLA Ops:
  7.2 88.2 %copy-start = (bf16[1024,19]{0,1:T(8,128)(2,1)S(1)}, bf16[1024,19]{0,1:T(8,128)(2,1)}, u32[]{:S(2)}) copy-start(bf16[1024,19]{0,1:T(8,128)(2,1)} %param.18) | copy-start | bytes 116740
  7.2 78.2 %all-gather.2.cloned.1.call-start = ((), (), s32[]{:S(2)}) async-start(), calls=%async_computation.1 | async-start | bytes 8912896 | tf_op jit(solution)/shard_map/all_gather | solution.py:97
  7.9 286.2 %reduce-scatter.2.cloned.1.call-start = ((), (), s32[]{:S(2)}) async-start(), calls=%async_computation.2 | async-start | bytes 17825792 | tf_op jit(solution)/shard_map/reduce_scatter | solution.py:125
  95.3 1.8 copy-start.4
  95.3 2.0 copy-start.6
  95.3 1.9 copy-start.7
  95.3 1.9 copy-start.8
  95.3 1.9 copy-start.9
  102.3 2.3 copy-start.5
  105.1 1.2 copy-start.1
  119.0 242.5 %all-reduce.19.cloned.1.call-start = ((), (), s32[]{:S(2)}) async-start(), calls=%async_computation.3 | async-start | bytes 2097152 | tf_op jit(solution)/shard_map/psum | solution.py:133
  294.1 173.7 %all-reduce.21.cloned.1.call-start = ((), (), s32[]{:S(2)}) async-start(), calls=%async_computation.4 | async-start | bytes 196608 | tf_op jit(solution)/shard_map/psum | solution.py:124
  307.6 11.1 %copy-start.2 = (f32[640,1024]{1,0:T(8,128)S(1)}, f32[640,1024]{1,0:T(8,128)}, u32[]{:S(2)}) copy-start(f32[640,1024]{1,0:T(8,128)} %get-tuple-element.39) | copy-start | bytes 7864324
  307.6 11.1 %copy-start.3 = (bf16[640,1024]{1,0:T(8,128)(2,1)S(1)}, bf16[640,1024]{1,0:T(8,128)(2,1)}, u32[]{:S(2)}) copy-start(bf16[640,1024]{1,0:T(8,128)(2,1)} %param.15) | copy-start | bytes 3932164
Sparse Core Ops, SparseCore 0:
  10.2 75.1 all-gather.1
  119.1 174.9 reduce-scatter.1
  296.4 40.8 all-reduce.18
  343.2 124.5 all-reduce.20
where the time goes:
time: 476 us
  waiting for transfers between devices  354 us (74%)
  matrix products  52.6 us (11%)
  blocking collectives  40.5 us (9%)
  between operations  14.1 us (3%)
  local copies, waits for them, and re-layouts  10.6 us (2%)
    reduce_scatter x1, waiting for transfers between devices, local(): lax.psum_scatter(lax.dot_general(learn_hidden, rounded, (((0,), (0,)), ((...  175 us
    psum x1, waiting for transfers between devices, local(): head_grad, gain_grad = lax.psum((head_local, gain_local), ('dp', 'rep'))  104 us
    all_gather x1, waiting for transfers between devices, local(): full_down = lax.all_gather(down_weight, 'dp', axis=0, tiled=True)  74.4 us
    psum x1, blocking collectives, local(): head_grad, gain_grad = lax.psum((head_local, gain_local), ('dp', 'rep'))  40.5 us
    dot_general x1, matrix products, local(): lax.dot_general(learn_hidden, rounded, (((0,), (0,)), ((), ())), preferre...  12.7 us
    dot_general x1, matrix products, local(): lax.dot_general(rounded, full_down, (((1,), (1,)), ((), ())), preferred_e...  11.1 us
    dot_general x1, matrix products, local(): jnp.dot(fresh_hidden, full_down, preferred_element_type=jnp.float32)  10.9 us
    dot_general x1, matrix products, local(): jnp.dot(learn_hidden, full_down, preferred_element_type=jnp.float32)  9.89 us
  transfers between devices with their start and end apart: 4, of which 3 were waited for; matrix products, arithmetic and copies ran while one was open for 7% of the time, Pallas kernels for 0%

commit v1 on v0

--- a/solution.py
+++ b/solution.py
@@ -1,3 +1,4 @@
+import functools
 import jax
 import jax.numpy as jnp
 from jax import lax
@@ -10,6 +11,15 @@
 BASELINE_COST = 0.5
 ENTROPY_COST = 0.05
 EPSILON = 1e-05
+
+
+def positions_settle(arr_in, device_axis, which_axis):
+    for num in (device_axis, which_axis):
+        arr_in = lax.psum(arr_in, num)
+    return arr_in
+
+
+meet_boxes = functools.partial(positions_settle, device_axis="rep", which_axis="dp")
 
 
 def normalize(features, gain_vector):
@@ -121,7 +131,7 @@
     )
     stream_grad, head_local, gain_local = pullback(jnp.ones_like(total_loss))
     rounded = stream_grad.astype(jnp.bfloat16)
-    head_grad, gain_grad = lax.psum((head_local, gain_local), ("dp", "rep"))
+    head_grad, gain_grad = meet_boxes((head_local, gain_local))
     grad_shard = lax.psum_scatter(
         lax.dot_general(
             learn_hidden, rounded, (((0,), (0,)), ((), ())), preferred_element_type=jnp.float32

time: 476 us -> 441 us (0.926)
  waiting for transfers between devices: 354 us -> 327 us
  blocking collectives: 40.5 us -> 29.4 us
    psum x1, waiting for transfers between devices: 104 us -> 56.3 us  [positions_settle(): arr_in = lax.psum(arr_in, num)]
    psum x1, waiting for transfers between devices: 0.01 us -> 34.2 us  [local(): down_grad = lax.psum(grad_shard, 'rep')]
    reduce_scatter x1, waiting for transfers between devices: 175 us -> 161 us  [local(): lax.psum_scatter(lax.dot_general(learn_hidden, rounded, (((0,), (0,)), ((...]
    psum x1 -> x2, blocking collectives: 40.5 us -> 29.4 us  [positions_settle(): arr_in = lax.psum(arr_in, num)]
  transfers between devices with their start and end apart: 4 -> 4, of which waited for: 3 -> 4; matrix products, arithmetic and copies ran while one was open for 7% -> 8% of each run, Pallas kernels for 0% -> 0%
where the time goes in v1:
time: 441 us; the launch traced here: 439 us
  waiting for transfers between devices  327 us (74%)
  matrix products  54 us (12%)
  blocking collectives  29.4 us (7%)
  between operations  14.1 us (3%)
  local copies, waits for them, and re-layouts  10.5 us (2%)
    reduce_scatter x1, waiting for transfers between devices, local(): lax.psum_scatter(lax.dot_general(learn_hidden, rounded, (((0,), (0,)), ((...  161 us
    all_gather x1, waiting for transfers between devices, local(): full_down = lax.all_gather(down_weight, 'dp', axis=0, tiled=True)  74.4 us
    psum x1, waiting for transfers between devices, positions_settle(): arr_in = lax.psum(arr_in, num)  56.3 us
    psum x1, waiting for transfers between devices, local(): down_grad = lax.psum(grad_shard, 'rep')  34.2 us
    psum x2, blocking collectives, positions_settle(): arr_in = lax.psum(arr_in, num)  29.4 us
    dot_general x1, matrix products, local(): lax.dot_general(learn_hidden, rounded, (((0,), (0,)), ((), ())), preferre...  12.7 us
    dot_general x1, matrix products, local(): lax.dot_general(rounded, full_down, (((1,), (1,)), ((), ())), preferred_e...  11.1 us
    dot_general x1, matrix products, local(): jnp.dot(fresh_hidden, full_down, preferred_element_type=jnp.float32)  11 us
  transfers between devices with their start and end apart: 4, of which 4 were waited for; matrix products, arithmetic and copies ran while one was open for 8% of the time, Pallas kernels for 0%

profile of v1, /device:TPU:8, one launch (start us, length us, event | category | flops | bytes accessed | tf_op | source)
XLA Modules:
  0.0 439.4 jit_solution(2903962940751762640)
XLA Ops:
  7.2 0.7 all-gather.2.cloned.1.call-update
  8.0 0.7 convert_element_type.21
  8.6 0.8 eq.12
  9.4 0.9 exponential_reduce_fusion
  10.3 0.7 broadcast_add_fusion
  10.9 74.4 %all-gather.2.cloned.1.call-done = bf16[4096,1024]{1,0:T(8,128)(2,1)} async-done(((bf16[256,1024]{1,0:T(8,128)(2,1)}), bf16[4096,1024]{1,0:T(8,128)(2,1)}) %all-gather.2.cloned.1.call-update) | async-done | bytes 8388624 | tf_op jit(solution)/shard_map/all_gather | solution.py:107
  85.4 9.9 %multiply_reduce_fusion.2 = (f32[640]{0:T(1024)S(1)}, f32[640,1024]{1,0:T(8,128)S(1)}) fusion(bf16[640,4096]{1,0:T(8,128)(2,1)} %param.14, bf16[4096,1024]{1,0:T(8,128)(2,1)} %all-gather.2.cloned.1.call-done, bf16[640,1024]{1,0:T(8,128)(2,1)} %param.13), kind=kOutput, calls=%fused_computation.6 | convolution fusion | flops 5371330048 | bytes 17566208 | tf_op jit(solution)/shard_map/dot_general | solution.py:108
  95.4 1.5 fusion.6
  97.4 0.1 slice.177
  97.5 0.1 slice.171
  97.6 0.1 slice.167
  97.7 0.1 slice.173
  97.8 0.1 slice.169
  100.2 0.1 slice.176
  100.3 0.1 slice.165
  102.0 0.1 pad.55
  102.7 1.8 multiply_reduce_fusion
  104.6 0.6 fusion
  105.2 1.1 copy-done.1
  106.2 12.7 %convolution_bitcast_fusion = f32[4096,1024]{0,1:T(8,128)} fusion(bf16[640,1024]{1,0:T(8,128)(2,1)S(1)} %fusion, bf16[640,4096]{1,0:T(8,128)(2,1)} %param.14), kind=kOutput, calls=%fused_computation | convolution fusion | flops 5368709120 | bytes 23330816 | tf_op jit(solution)/shard_map/dot_general | solution.py:136
  119.0 0.2 all-reduce.22.cloned.1.call-start
  119.2 11.0 %multiply_reduce_fusion.3 = (f32[640]{0:T(1024)S(1)}, f32[640,1024]{1,0:T(8,128)}) fusion(bf16[640,1024]{1,0:T(8,128)(2,1)} %param.15, bf16[640,4096]{1,0:T(8,128)(2,1)} %param.16, bf16[4096,1024]{1,0:T(8,128)(2,1)} %all-gather.2.cloned.1.call-done), kind=kOutput, calls=%fused_computation.11 | convolution fusion | flops 5371330048 | bytes 17566208 | tf_op jit(solution)/shard_map/dot_general | solution.py:111
  130.2 2.4 fusion.4
  132.6 161.5 %reduce-scatter.2.cloned.1.call-done = f32[256,1024]{0,1:T(8,128)} async-done(((f32[4096,1024]{0,1:T(8,128)}), f32[256,1024]{0,1:T(8,128)}) %reduce-scatter.2.cloned.1.call-update) | async-done | bytes 1048592 | tf_op jit(solution)/shard_map/reduce_scatter | solution.py:135
  294.2 11.1 %convolution_convert_fusion = bf16[640,4096]{1,0:T(8,128)(2,1)} fusion(bf16[640,1024]{1,0:T(8,128)(2,1)} %copy-done.1, bf16[4096,1024]{1,0:T(8,128)(2,1)} %all-gather.2.cloned.1.call-done), kind=kOutput, calls=%fused_computation.1 | convolution fusion | flops 5371330560 | bytes 14942208 | tf_op jit(solution)/shard_map/dot_general | solution.py:144
  305.2 34.2 %all-reduce.22.cloned.1.call-done = (f32[256,1024]{0,1:T(8,128)}, f32[1024,19]{0,1:T(8,128)}) async-done(((f32[256,1024]{0,1:T(8,128)}, f32[1024,19]{0,1:T(8,128)}), (f32[256,1024]{0,1:T(8,128)}, f32[1024,19]{0,1:T(8,128)})) %all-reduce.22.cloned.1.call-update) | async-done | bytes 1126416 | tf_op jit(solution)/shard_map/psum | solution.py:143
  339.5 3.6 fusion.1
  343.1 4.9 %psum.38 = f32[1024]{0:T(1024)S(1)} all-reduce(f32[1024]{0:T(1024)S(1)} %get-tuple-element.12), channel_id=1, replica_groups=mesh['dp'=16,'rep'=2] {'rep'}, use_global_device_ids=true, to_apply=%region_13.14 | all-reduce | flops 1024 | bytes 8192 | tf_op jit(solution)/shard_map/psum | solution.py:18
  348.0 24.5 %psum.39 = f32[1024]{0:T(1024)} all-reduce(f32[1024]{0:T(1024)S(1)} %psum.38), channel_id=1, replica_groups=mesh['dp'=16,'rep'=2] {'dp'}, use_global_device_ids=true, to_apply=%region_14.15 | all-reduce | flops 1024 | bytes 8192 | tf_op jit(solution)/shard_map/psum | solution.py:18
  372.5 2.5 copy.19
  375.1 56.3 %all-reduce.20.cloned.1.call-done = f32[1024,19]{0,1:T(8,128)} async-done(((f32[1024,19]{0,1:T(8,128)}), f32[1024,19]{0,1:T(8,128)}) %all-reduce.20.cloned.1.call-update) | async-done | bytes 77840 | tf_op jit(solution)/shard_map/psum | solution.py:18
  431.4 1.5 copy.23
  (106 shorter events, 5.0 us)
Async XLA Ops:
  7.2 88.2 %copy-start = (bf16[1024,19]{0,1:T(8,128)(2,1)S(1)}, bf16[1024,19]{0,1:T(8,128)(2,1)}, u32[]{:S(2)}) copy-start(bf16[1024,19]{0,1:T(8,128)(2,1)} %param.18) | copy-start | bytes 116740
  7.2 78.2 %all-gather.2.cloned.1.call-start = ((), (), s32[]{:S(2)}) async-start(), calls=%async_computation.1 | async-start | bytes 8912896 | tf_op jit(solution)/shard_map/all_gather | solution.py:107
  7.9 286.2 %reduce-scatter.2.cloned.1.call-start = ((), (), s32[]{:S(2)}) async-start(), calls=%async_computation.2 | async-start | bytes 17825792 | tf_op jit(solution)/shard_map/reduce_scatter | solution.py:135
  95.3 1.8 copy-start.3
  95.3 2.0 copy-start.5
  95.3 1.9 copy-start.6
  95.3 1.9 copy-start.7
  95.3 1.9 copy-start.8
  102.3 2.3 copy-start.4
  105.2 1.1 copy-start.1
  119.0 220.5 %all-reduce.22.cloned.1.call-start = ((), (), s32[]{:S(2)}) async-start(), calls=%async_computation.4 | async-start | bytes 2293760 | tf_op jit(solution)/shard_map/psum | solution.py:143
  294.1 45.4 %copy-start.2 = (f32[640,1024]{1,0:T(8,128)S(1)}, f32[640,1024]{1,0:T(8,128)}, u32[]{:S(2)}) copy-start(f32[640,1024]{1,0:T(8,128)} %get-tuple-element.41) | copy-start | bytes 7864324
  294.1 137.3 %all-reduce.20.cloned.1.call-start = ((), (), s32[]{:S(2)}) async-start(), calls=%async_computation.3 | async-start | bytes 196608 | tf_op jit(solution)/shard_map/psum | solution.py:18
Sparse Core Ops, SparseCore 0:
  10.2 75.1 all-gather.1
  119.1 174.9 reduce-scatter.1
  297.1 42.3 all-reduce.21
  342.7 88.5 all-reduce.19
